TPU v7x, 32 devices: a whole 2x2x4 slice. The times are simulated.
32 devices in a mesh: row: 4 (over z), col: 2 (over x), rep: 4 (over y, core).
Axes of the slice: x: 2, y: 2, z: 4, core: 2. Of those that a mesh axis runs over, the one named last changes fastest.
Arguments:
- density: bfloat16 [1536, 1536], P('row', 'col'), as said below
- keep_square: int32 [12, 12], P('row', 'col'), may hold values 0 or 1
- keep_cube: int32 [12, 12], P('row', 'col'), may hold values 0 or 1
Outputs:
- purified: float32 [1536, 1536], P(('row', 'rep'), 'col')
Inputs may be any that keep to these rules, and one draw needn't show every extreme that they name: density is symmetric; its 128 x 128 diagonal blocks are always occupied, any other block may be zero or occupied at any distance from the diagonal.
All inputs are finite; a program needn't handle non-finite values. No bound on the sum of `keep_square` or of `keep_cube` on one device may be relied on, other than what follows from the above.
Results may differ from a plain program's by a relative error of at most 0.002.
Values may be sent and summed in bfloat16 or wider, within the bound.
A program may use at most 64 MiB of HBM per device.

v0:
```python
import jax
import jax.numpy as jnp
from jax import lax
from jax.sharding import PartitionSpec as P

BLK = 128


def broadcast(array, axis, root):
    mine = lax.axis_index(axis) == root
    return lax.psum(jnp.where(mine, array, jnp.zeros_like(array)), axis)


def widen(mask, tile_rows, tile_cols):
    blocks = jnp.broadcast_to(
        mask.astype(jnp.float32)[:, None, :, None], (mask.shape[0], BLK, mask.shape[1], BLK)
    )
    return blocks.reshape(tile_rows, tile_cols)


def left_piece(tile, piece_index):
    height = tile.shape[0]
    per_tile = tile.shape[1] // height
    column = lax.dynamic_slice_in_dim(tile, piece_index % per_tile * height, height, 1)
    return broadcast(column, "col", piece_index // per_tile)


def right_piece(density, piece_index):
    return broadcast(density, "row", piece_index)


def local(density, keep_square, keep_cube):
    tile_rows, tile_cols = density.shape
    rep_count = lax.axis_size("rep")
    row_count = lax.axis_size("row")
    rep_index = lax.axis_index("rep")
    sections = row_count // rep_count
    indices = [position * rep_count + rep_index for position in range(sections)]
    square_total = jnp.zeros((tile_rows, tile_cols), jnp.float32)
    for piece_index in indices:
        right_panel = right_piece(density, piece_index)
        square_total = square_total + jnp.dot(
            left_piece(density, piece_index), right_panel, preferred_element_type=jnp.float32
        )
    square_total = square_total * widen(keep_square, tile_rows, tile_cols)
    square_own = lax.psum_scatter(square_total, "rep", scatter_dimension=0, tiled=True)
    square_low = lax.all_gather(square_own.astype(jnp.bfloat16), "rep", axis=0, tiled=True)
    cube_total = jnp.zeros((tile_rows, tile_cols), jnp.float32)
    for number, piece_index in enumerate(indices):
        right_panel = right_piece(density, piece_index)
        cube_total = cube_total + jnp.dot(
            left_piece(square_low, piece_index), right_panel, preferred_element_type=jnp.float32
        )
    cube_total = cube_total * widen(keep_cube, tile_rows, tile_cols)
    cube_own = lax.psum_scatter(cube_total, "rep", scatter_dimension=0, tiled=True)
    return 3.0 * square_own - 2.0 * cube_own


def solution(mesh):
    return jax.shard_map(
        local,
        mesh=mesh,
        in_specs=(P("row", "col"), P("row", "col"), P("row", "col")),
        out_specs=P(("row", "rep"), "col"),
        check_vma=False,
    )
```

profile of v0, /device:TPU:0, one launch (start us, length us, event | category | flops | bytes accessed | tf_op | source)
XLA Modules:
  0.0 175.6 jit_solution(14447856597460182150)
XLA Ops:
  6.5 0.0 all-reduce.4.cloned.1.call-start
  6.5 1.8 %dynamic-slice_select_fusion.1 = bf16[384,384]{1,0:T(8,128)(2,1)} fusion(bf16[384,768]{1,0:T(8,128)(2,1)} %param.3, s32[]{:T(128)S(6)} %select_n.43, pred[]{:T(512)S(6)} %eq.11), kind=kLoop, calls=%fused_computation.5 | loop fusion | flops 147456 | bytes 589829 | tf_op jit(solution)/shard_map/jit(_where)/select_n | solution.py:11
  8.3 0.0 all-reduce.4.cloned.1.call-update
  8.4 0.0 all-reduce.6.cloned.1.call-start
  8.4 0.0 copy-done.1
  8.4 0.9 broadcast_select_fusion
  9.3 0.0 all-reduce.6.cloned.1.call-update
  9.3 0.0 reduce-scatter.3.cloned.1.call-start
  9.4 0.0 copy-done.5
  9.4 26.7 %all-reduce.4.cloned.1.call-done = bf16[384,384]{1,0:T(8,128)(2,1)} async-done(((bf16[384,384]{1,0:T(8,128)(2,1)}), bf16[384,384]{1,0:T(8,128)(2,1)}) %all-reduce.4.cloned.1.call-update) | async-done | bytes 294928 | tf_op jit(solution)/shard_map/psum | solution.py:11
  36.1 42.0 %all-reduce.6.cloned.1.call-done = bf16[384,768]{1,0:T(8,128)(2,1)} async-done(((bf16[384,768]{1,0:T(8,128)(2,1)}), bf16[384,768]{1,0:T(8,128)(2,1)}) %all-reduce.6.cloned.1.call-update) | async-done | bytes 589840 | tf_op jit(solution)/shard_map/psum | solution.py:11
  78.1 0.2 broadcast_in_dim.4
  78.3 0.0 copy-done.3
  78.3 0.9 copy-done
  79.2 1.5 convolution_multiply_fusion.1
  80.7 0.0 reduce-scatter.3.cloned.1.call-update
  80.7 0.0 copy-start.6
  80.7 0.0 all-reduce.8.cloned.1.call-start
  80.8 25.2 %reduce-scatter.3.cloned.1.call-done = f32[96,768]{1,0:T(8,128)} async-done(((f32[384,768]{1,0:T(8,128)}), f32[96,768]{1,0:T(8,128)}) %reduce-scatter.3.cloned.1.call-update) | async-done | bytes 294928 | tf_op jit(solution)/shard_map/reduce_scatter | solution.py:46
  105.9 1.0 convert_element_type.10
  106.9 6.9 %all_gather.3 = bf16[384,768]{1,0:T(8,128)(2,1)S(1)} all-gather(bf16[96,768]{1,0:T(8,128)(2,1)S(1)} %convert_element_type.10), channel_id=1, replica_groups=mesh['row'=4,'col'=2,'rep'=4] {'rep'}, dimensions={0}, use_global_device_ids=true | all-gather | bytes 737280 | tf_op jit(solution)/shard_map/all_gather | solution.py:47
  113.9 0.8 dynamic-slice_select_fusion
  114.6 0.0 all-reduce.8.cloned.1.call-update
  114.7 0.0 reduce-scatter.5.cloned.1.call-start
  114.7 0.0 copy-done.6
  114.7 24.3 %all-reduce.8.cloned.1.call-done = bf16[384,384]{1,0:T(8,128)(2,1)} async-done(((bf16[384,384]{1,0:T(8,128)(2,1)}), bf16[384,384]{1,0:T(8,128)(2,1)}) %all-reduce.8.cloned.1.call-update) | async-done | bytes 294928 | tf_op jit(solution)/shard_map/psum | solution.py:11
  139.1 0.2 broadcast_in_dim.5
  139.2 0.8 copy-done.4
  140.0 1.5 convolution_multiply_fusion
  141.5 0.0 reduce-scatter.5.cloned.1.call-update
  141.5 25.8 %reduce-scatter.5.cloned.1.call-done = f32[96,768]{1,0:T(8,128)} async-done(((f32[384,768]{1,0:T(8,128)}), f32[96,768]{1,0:T(8,128)}) %reduce-scatter.5.cloned.1.call-update) | async-done | bytes 294928 | tf_op jit(solution)/shard_map/reduce_scatter | solution.py:55
  167.3 1.7 multiply_subtract_fusion
  (9 shorter events, 0.0 us)
Async XLA Ops:
  6.5 1.9 %copy-start.1 = (bf16[384,768]{1,0:T(8,128)(2,1)S(1)}, bf16[384,768]{1,0:T(8,128)(2,1)}, u32[]{:S(2)}) copy-start(bf16[384,768]{1,0:T(8,128)(2,1)} %param.3) | copy-start | bytes 1769476
  6.5 29.5 %all-reduce.4.cloned.1.call-start = ((), (), s32[]{:S(2)}) async-start(), calls=%async_computation.2 | async-start | bytes 589824 | tf_op jit(solution)/shard_map/psum | solution.py:11
  8.3 1.0 copy-start.5
  8.4 69.7 %all-reduce.6.cloned.1.call-start = ((), (), s32[]{:S(2)}) async-start(), calls=%async_computation.3 | async-start | bytes 1179648 | tf_op jit(solution)/shard_map/psum | solution.py:11
  9.3 96.6 %reduce-scatter.3.cloned.1.call-start = ((), (), s32[]{:S(2)}) async-start(), calls=%async_computation.4 | async-start | bytes 1474560 | tf_op jit(solution)/shard_map/reduce_scatter | solution.py:46
  36.1 42.2 %copy-start.3 = (bf16[384,384]{1,0:T(8,128)(2,1)S(1)}, bf16[384,384]{1,0:T(8,128)(2,1)}, u32[]{:S(2)}) copy-start(bf16[384,384]{1,0:T(8,128)(2,1)} %all-reduce.4.cloned.1.call-done) | copy-start | bytes 884740
  78.1 1.1 copy-start
  80.7 34.0 %copy-start.6 = (s32[3,6]{1,0:T(4,128)S(1)}, s32[3,6]{1,0:T(4,128)}, u32[]{:S(2)}) copy-start(s32[3,6]{1,0:T(4,128)} %param.5) | copy-start | bytes 220
  80.7 58.4 %all-reduce.8.cloned.1.call-start = ((), (), s32[]{:S(2)}) async-start(), calls=%async_computation.5 | async-start | bytes 589824 | tf_op jit(solution)/shard_map/psum | solution.py:11
  114.7 52.7 %reduce-scatter.5.cloned.1.call-start = ((), (), s32[]{:S(2)}) async-start(), calls=%async_computation.6 | async-start | bytes 1474560 | tf_op jit(solution)/shard_map/reduce_scatter | solution.py:55
  139.1 1.0 copy-start.4
  141.5 25.8 %copy-start.2 = (f32[96,768]{1,0:T(8,128)S(1)}, f32[96,768]{1,0:T(8,128)}, u32[]{:S(2)}) copy-start(f32[96,768]{1,0:T(8,128)} %reduce-scatter.3.cloned.1.call-done) | copy-start | bytes 884740
Sparse Core Ops, SparseCore 0:
  9.6 26.4 all-reduce.3
  38.4 39.6 all-reduce.5
  80.8 25.0 reduce-scatter.2
  114.8 24.2 all-reduce.7
  141.7 25.6 reduce-scatter.4
where the time goes:
time: 176 us
  waiting for transfers between devices  144 us (82%)
  between operations  13.2 us (8%)
  blocking collectives  6.95 us (4%)
  other arithmetic  6.12 us (3%)
  matrix products  3 us (2%)
  local copies, waits for them, and re-layouts  2.03 us (1%)
    psum x3, waiting for transfers between devices, broadcast(): return lax.psum(jnp.where(mine, array, jnp.zeros_like(array)), axis)  93 us
    reduce_scatter x1, waiting for transfers between devices, local(): lax.psum_scatter(cube_total, 'rep', scatter_dimension=0, tiled=True)  25.8 us
    reduce_scatter x1, waiting for transfers between devices, local(): lax.psum_scatter(square_total, 'rep', scatter_dimension=0, tiled=True)  25.2 us
    all_gather x1, blocking collectives, local(): lax.all_gather(square_own.astype(jnp.bfloat16), 'rep', axis=0, tiled=True)  6.95 us
  transfers between devices with their start and end apart: 5, of which 5 were waited for; matrix products, arithmetic and copies ran while one was open for 0% of the time, Pallas kernels for 0%

commit v1 on v0

--- a/solution.py
+++ b/solution.py
@@ -6,9 +6,14 @@
 BLK = 128
 
 
+def run_the_samples(load, axis_name):
+    lower = jax.lax.all_gather(load, axis_name=axis_name)
+    return jnp.sum(lower, axis=0)
+
+
 def broadcast(array, axis, root):
     mine = lax.axis_index(axis) == root
-    return lax.psum(jnp.where(mine, array, jnp.zeros_like(array)), axis)
+    return run_the_samples(jnp.where(mine, array, jnp.zeros_like(array)), axis)
 
 
 def widen(mask, tile_rows, tile_cols):

time: 176 us -> 145 us (0.82)
  waiting for transfers between devices: 144 us -> 93.1 us
  blocking collectives: 6.95 us -> 26.6 us
    psum x3 -> x0, waiting for transfers between devices: 93 us -> none  [broadcast(): return lax.psum(jnp.where(mine, array, jnp.zeros_like(array)), axis)]
    all_gather x0 -> x1, waiting for transfers between devices: none -> 42.9 us  [run_the_samples(): lower = jax.lax.all_gather(load, axis_name=axis_name)]
    all_gather x0 -> x2, blocking collectives: none -> 19.7 us  [run_the_samples(): lower = jax.lax.all_gather(load, axis_name=axis_name)]
    reduce_sum x0 -> x3, other arithmetic: none -> 2.65 us  [run_the_samples(): return jnp.sum(lower, axis=0)]
  transfers between devices with their start and end apart: 5 -> 3, of which waited for: 5 -> 3; matrix products, arithmetic and copies ran while one was open for 0% -> 0% of each run, Pallas kernels for 0% -> 0%
where the time goes in v1:
time: 145 us; the launch traced here: 144 us
  waiting for transfers between devices  93.1 us (64%)
  blocking collectives  26.6 us (18%)
  between operations  13.2 us (9%)
  other arithmetic  7.47 us (5%)
  matrix products  2.98 us (2%)
    all_gather x1, waiting for transfers between devices, run_the_samples(): lower = jax.lax.all_gather(load, axis_name=axis_name)  42.9 us
    reduce_scatter x1, waiting for transfers between devices, local(): lax.psum_scatter(cube_total, 'rep', scatter_dimension=0, tiled=True)  26.3 us
    reduce_scatter x1, waiting for transfers between devices, local(): lax.psum_scatter(square_total, 'rep', scatter_dimension=0, tiled=True)  23.9 us
    all_gather x2, blocking collectives, run_the_samples(): lower = jax.lax.all_gather(load, axis_name=axis_name)  19.7 us
    all_gather x1, blocking collectives, local(): lax.all_gather(square_own.astype(jnp.bfloat16), 'rep', axis=0, tiled=True)  6.96 us
  transfers between devices with their start and end apart: 3, of which 3 were waited for; matrix products, arithmetic and copies ran while one was open for 0% of the time, Pallas kernels for 0%

profile of v1, /device:TPU:0, one launch (start us, length us, event | category | flops | bytes accessed | tf_op | source)
XLA Modules:
  0.0 144.5 jit_solution(9834058554268184638)
XLA Ops:
  6.5 0.0 copy-start
  6.5 0.0 copy-start.2
  6.5 0.0 all-gather.5.cloned.1.call-start
  6.5 2.0 %broadcast_select_fusion = bf16[384,768]{1,0:T(8,128)(2,1)} fusion(bf16[384,768]{1,0:T(8,128)(2,1)} %param.3, pred[]{:T(512)S(6)} %eq.12), kind=kLoop, calls=%fused_computation.2 | loop fusion | flops 294912 | bytes 1179649 | tf_op jit(solution)/shard_map/jit(_where)/select_n | solution.py:16
  8.5 0.0 all-gather.5.cloned.1.call-update
  8.6 0.0 reduce-scatter.3.cloned.1.call-start
  8.6 0.0 copy-done.2
  8.7 0.0 copy-done
  8.7 0.1 dynamic-slice_select_fusion.1
  8.8 9.8 %all-gather = bf16[768,384]{1,0:T(8,128)(2,1)S(1)} all-gather(bf16[384,384]{1,0:T(8,128)(2,1)S(1)} %dynamic-slice_select_fusion.1), channel_id=2, replica_groups=mesh['row'=4,'col'=2,'rep'=4] {'col'}, dimensions={0}, use_global_device_ids=true | all-gather | bytes 884736 | tf_op jit(solution)/shard_map/all_gather | solution.py:10
  18.5 0.2 reduce_sum.40
  18.7 42.9 %all-gather.5.cloned.1.call-done = bf16[1536,768]{1,0:T(8,128)(2,1)} async-done(((bf16[384,768]{1,0:T(8,128)(2,1)}), bf16[1536,768]{1,0:T(8,128)(2,1)}) %all-gather.5.cloned.1.call-update) | async-done | bytes 2359312 | tf_op jit(solution)/shard_map/all_gather | solution.py:10
  61.6 2.3 %reduce_sum.41 = bf16[384,768]{1,0:T(8,128)(2,1)S(1)} reduce(bf16[4,384,768]{2,1,0:T(8,128)(2,1)} %bitcast.17, bf16[]{:T(256)} %constant.53.clone.1), dimensions={0}, to_apply=%region_1.2 | reduce | flops 884736 | bytes 2949122 | tf_op jit(solution)/shard_map/reduce_sum | solution.py:11
  64.0 0.2 broadcast_in_dim.4
  64.1 1.5 %convolution_multiply_fusion.1 = f32[384,768]{1,0:T(8,128)} fusion(bf16[384,384]{1,0:T(8,128)(2,1)S(1)} %reduce_sum.40, bf16[384,768]{1,0:T(8,128)(2,1)S(1)} %reduce_sum.41, f32[48,8,6,128]{3,2,1,0:T(8,128)S(1)} %bitcast.16), kind=kOutput, calls=%fused_computation.1 | convolution fusion | flops 226787328 | bytes 3244032 | tf_op jit(solution)/shard_map/dot_general | solution.py:47
  65.6 0.0 copy-start.3
  65.6 0.0 reduce-scatter.3.cloned.1.call-update
  65.6 0.0 reduce-scatter.5.cloned.1.call-start
  65.7 0.6 copy-done.3
  66.3 23.9 %reduce-scatter.3.cloned.1.call-done = f32[96,768]{1,0:T(8,128)} async-done(((f32[384,768]{1,0:T(8,128)}), f32[96,768]{1,0:T(8,128)}) %reduce-scatter.3.cloned.1.call-update) | async-done | bytes 294928 | tf_op jit(solution)/shard_map/reduce_scatter | solution.py:51
  90.2 1.0 convert_element_type.7
  91.1 7.0 %all_gather.27 = bf16[384,768]{1,0:T(8,128)(2,1)S(1)} all-gather(bf16[96,768]{1,0:T(8,128)(2,1)S(1)} %convert_element_type.7), channel_id=1, replica_groups=mesh['row'=4,'col'=2,'rep'=4] {'rep'}, dimensions={0}, use_global_device_ids=true | all-gather | bytes 737280 | tf_op jit(solution)/shard_map/all_gather | solution.py:52
  98.1 0.1 dynamic-slice_select_fusion
  98.2 9.9 %all-gather.2 = bf16[768,384]{1,0:T(8,128)(2,1)S(1)} all-gather(bf16[384,384]{1,0:T(8,128)(2,1)S(1)} %dynamic-slice_select_fusion), channel_id=4, replica_groups=mesh['row'=4,'col'=2,'rep'=4] {'col'}, dimensions={0}, use_global_device_ids=true | all-gather | bytes 884736 | tf_op jit(solution)/shard_map/all_gather | solution.py:10
  108.1 0.2 reduce_sum.42
  108.3 0.2 broadcast_in_dim.5
  108.4 1.5 %convolution_multiply_fusion = f32[384,768]{1,0:T(8,128)} fusion(bf16[384,384]{1,0:T(8,128)(2,1)S(1)} %reduce_sum.42, bf16[384,768]{1,0:T(8,128)(2,1)S(1)} %reduce_sum.41, f32[48,8,6,128]{3,2,1,0:T(8,128)S(1)} %bitcast.15), kind=kOutput, calls=%fused_computation | convolution fusion | flops 226787328 | bytes 3244032 | tf_op jit(solution)/shard_map/dot_general | solution.py:56
  109.9 0.0 copy-start.1
  109.9 0.0 reduce-scatter.5.cloned.1.call-update
  110.0 26.3 %reduce-scatter.5.cloned.1.call-done = f32[96,768]{1,0:T(8,128)} async-done(((f32[384,768]{1,0:T(8,128)}), f32[96,768]{1,0:T(8,128)}) %reduce-scatter.5.cloned.1.call-update) | async-done | bytes 294928 | tf_op jit(solution)/shard_map/reduce_scatter | solution.py:60
  136.3 0.0 copy-done.1
  136.3 1.7 %multiply_subtract_fusion = f32[96,768]{1,0:T(8,128)} fusion(f32[96,768]{1,0:T(8,128)} %reduce-scatter.5.cloned.1.call-done, f32[96,768]{1,0:T(8,128)S(1)} %copy-done.1), kind=kLoop, calls=%fused_computation.3 | loop fusion | flops 221184 | bytes 884736 | tf_op jit(solution)/shard_map/sub | solution.py:61
  (2 shorter events, 0.0 us)
Async XLA Ops:
  6.5 2.2 %copy-start = (bf16[384,768]{1,0:T(8,128)(2,1)S(1)}, bf16[384,768]{1,0:T(8,128)(2,1)}, u32[]{:S(2)}) copy-start(bf16[384,768]{1,0:T(8,128)(2,1)} %param.3) | copy-start | bytes 1769476
  6.5 2.1 %copy-start.2 = (s32[3,6]{1,0:T(4,128)S(1)}, s32[3,6]{1,0:T(4,128)}, u32[]{:S(2)}) copy-start(s32[3,6]{1,0:T(4,128)} %param.4) | copy-start | bytes 220
  6.5 55.1 %all-gather.5.cloned.1.call-start = ((), (), s32[]{:S(2)}) async-start(), calls=%async_computation.4 | async-start | bytes 2949120 | tf_op jit(solution)/shard_map/all_gather | solution.py:10
  8.6 81.6 %reduce-scatter.3.cloned.1.call-start = ((), (), s32[]{:S(2)}) async-start(), calls=%async_computation.2 | async-start | bytes 1474560 | tf_op jit(solution)/shard_map/reduce_scatter | solution.py:51
  65.6 0.7 copy-start.3
  65.6 70.6 %reduce-scatter.5.cloned.1.call-start = ((), (), s32[]{:S(2)}) async-start(), calls=%async_computation.3 | async-start | bytes 1474560 | tf_op jit(solution)/shard_map/reduce_scatter | solution.py:60
  109.9 26.3 %copy-start.1 = (f32[96,768]{1,0:T(8,128)S(1)}, f32[96,768]{1,0:T(8,128)}, u32[]{:S(2)}) copy-start(f32[96,768]{1,0:T(8,128)} %reduce-scatter.3.cloned.1.call-done) | copy-start | bytes 884740
Sparse Core Ops, SparseCore 0:
  8.9 52.6 all-gather.4
  65.8 24.3 reduce-scatter.2
  110.1 26.1 reduce-scatter.4
